TPU v7x, 256 devices: a whole 4x4x8 slice. The times are simulated.
256 devices in a mesh: rows: 64 (over z, x, core), grp: 4 (over y).
Axes of the slice: x: 4, y: 4, z: 8, core: 2. Of those that a mesh axis runs over, the one named last changes fastest.
Arguments:
- observations: float32 [524288, 512], P(('rows', 'grp')), may hold values from -32 to 32, as said below
- sensor_ids: int32 [524288], P(('rows', 'grp')), may hold values from 0 to 127
- sensor_sigma: float32 [128], replicated, may hold values from 0.3 to 3
- buckets: int32 [524288], P(('rows', 'grp')), may hold values from 0 to 63, as said below
- prior_factor: float32 [512, 512], replicated, may hold values from -0.3 to 3, as said below
Outputs:
- whitened: float32 [524288, 512], P(('rows', 'grp'))
- info_factor: float32 [512, 512], replicated
Inputs may be any that keep to these rules, and one draw needn't show every extreme that they name: `buckets`: in each aligned block of 2048 rows every bucket index appears exactly 32 times. `observations`: rows are real-valued without further structure. `prior_factor`: upper triangular with a positive diagonal of at least 0.5.
All inputs are finite; a program needn't handle non-finite values.
Results may differ from a plain program's by a relative error of at most 0.00007.
Values sent between devices are 32-bit elements; how exact they have to be, the bound alone decides.
A program may use at most 128 MiB of HBM per device.

v0:
```python
import jax
import jax.numpy as jnp
from jax import lax
from jax.sharding import PartitionSpec as P


def matmul(left, right):
    return jnp.dot(left, right, precision=lax.Precision.HIGHEST, preferred_element_type=jnp.float32)


def outer_sum(values):
    return lax.dot_general(
        values,
        values,
        (((0,), (0,)), ((), ())),
        precision=lax.Precision.HIGHEST,
        preferred_element_type=jnp.float32,
    )


def square_form(matrix):
    return matmul(matrix.T, matrix)


def lower_inverse(lower):
    width = lower.shape[0]
    identity = jnp.eye(width, dtype=jnp.float32)
    diag_values = jnp.diagonal(lower)
    scaled_lower = lower / diag_values[:, None]
    nilpotent = identity - scaled_lower
    product = identity + nilpotent
    power = nilpotent
    reach = 2
    while reach < width:
        power = matmul(power, power)
        product = product + matmul(product, power)
        reach = reach * 2
    return product / diag_values[None, :]


def upper_factor(matrix):
    return jnp.linalg.cholesky(matrix).T


def whiten_rows(values, factor):
    inverse = lower_inverse(factor.T)
    return matmul(values, inverse.T)


def regroup_rows(values, target):
    outgoing = jnp.zeros_like(values).at[target].set(values)
    return lax.all_to_all(outgoing, "rows", split_axis=0, concat_axis=0, tiled=True)


def reduce_gram(local_gram, prior_gram, total_rows):
    summed = lax.psum(local_gram, ("rows", "grp"))
    return upper_factor(prior_gram + summed / jnp.float32(total_rows))


def shards(observations, sensor_ids, sensor_sigma, buckets, prior_factor):
    rows_dev = observations.shape[0]
    row_groups = lax.axis_size("rows")
    devices = lax.axis_size(("rows", "grp"))
    per_bucket = rows_dev // row_groups
    total_rows = rows_dev * devices
    inv_sigma = 1.0 / sensor_sigma
    matches = sensor_ids[:, None] == jnp.arange(sensor_sigma.shape[0], dtype=jnp.int32)[None, :]
    row_scale = jnp.sum(jnp.where(matches, inv_sigma[None, :], jnp.float32(0.0)), axis=1)
    scaled = observations * row_scale[:, None]
    onehot = (buckets[:, None] == jnp.arange(row_groups, dtype=jnp.int32)[None, :]).astype(
        jnp.int32
    )
    running = jnp.cumsum(onehot, axis=0)
    within = jnp.sum(onehot * running, axis=1) - 1
    target = buckets * per_bucket + within
    prior_gram = square_form(prior_factor)
    received = regroup_rows(scaled, target)
    factor = reduce_gram(outer_sum(received), prior_gram, total_rows)
    whitened = whiten_rows(received, factor)
    return (whitened, factor)


def solution(mesh):
    in_specs = (P(("rows", "grp"), None), P(("rows", "grp")), P(), P(("rows", "grp")), P())
    out_specs = (P(("rows", "grp"), None), P())
    return jax.shard_map(shards, mesh=mesh, in_specs=in_specs, out_specs=out_specs, check_vma=False)
```

profile of v0, /device:TPU:2, one launch (start us, length us, event | category | flops | bytes accessed | tf_op | source)
XLA Modules:
  0.0 560.0 jit_solution(9048692939131870598)
XLA Ops:
  7.2 0.7 broadcast_divide_fusion
  8.0 0.7 fusion.8
  8.7 18.1 %reduce-window.6 = s32[64,16,128]{2,1,0:T(8,128)S(1)} reduce-window(s32[64,16,128]{2,1,0:T(8,128)S(1)} %fusion.8, s32[]{:T(128)} %constant.151.clone.1), window={size=1x1x128 pad=0_0x0_0x127_0}, to_apply=%region_0.1 | reduce-window | flops 16646144 | bytes 1048580 | tf_op jit(solution)/shard_map/reduce-window
  27.1 0.4 copy.35
  28.1 0.6 select_reduce_fusion
  28.8 13.0 %scatter_custom_fusion = f32[2048,512]{1,0:T(8,128)} fusion(s32[2048]{0:T(1024)S(1)} %compare_select_fusion, f32[2048,512]{1,0:T(8,128)} %param.5, f32[2048]{0:T(1024)S(1)} %select_reduce_fusion, f32[]{:T(128)} %constant.149.clone.1), kind=kCustom, calls=%fused_computation.2 | custom fusion | flops 1048576 | bytes 8396804 | tf_op jit(solution)/shard_map/scatter | solution.py:51
  41.7 108.2 %all_to_all.12 = f32[64,32,512]{2,1,0:T(8,128)S(1)} all-to-all(f32[64,32,512]{2,1,0:T(8,128)} %bitcast.84), channel_id=1, replica_groups=mesh['rows'=64,'grp'=4] {'rows'}, dimensions={0} | all-to-all | bytes 8388608 | tf_op jit(solution)/shard_map/all_to_all | solution.py:52
  149.9 2.0 copy-done.1
  152.0 8.0 %convolution_bitcast_fusion = f32[512,512]{0,1:T(8,128)} fusion(f32[64,32,512]{2,1,0:T(8,128)S(1)} %all_to_all.12), kind=kOutput, calls=%fused_computation.17 | convolution fusion | flops 6442450944 | bytes 5242880 | tf_op jit(solution)/shard_map/dot_general | solution.py:12
  160.0 252.4 %all-reduce.3.cloned.1.call-done = f32[512,512]{0,1:T(8,128)} async-done(((f32[512,512]{0,1:T(8,128)}), f32[512,512]{0,1:T(8,128)}) %all-reduce.3.cloned.1.call-update) | async-done | bytes 1048592 | tf_op jit(solution)/shard_map/psum | solution.py:56
  412.5 3.1 convolution_add_fusion.8
  415.6 0.3 copy.31
  416.2 1.0 copy-done.3
  417.1 12.2 %cholesky.104 = f32[128,128]{1,0:T(8,128)S(1)} custom-call(f32[128,128]{1,0:T(8,128)S(1)} %cholesky.266), custom_call_target="Cholesky" | custom-call | tf_op jit(solution)/shard_map/jit(cholesky)/cholesky | solution.py:42
  429.5 9.8 %custom-call.27 = f32[1,128,128]{1,2,0:T(8,128)S(1)} custom-call(f32[1,128,128]{2,1,0:T(8,128)S(1)} %get-tuple-element.19), custom_call_target="InvertDiagBlocksLowerTriangular" | custom-call | tf_op jit(solution)/shard_map/jit(cholesky)/cholesky | solution.py:42
  439.3 1.2 constant_dynamic-update-slice_fusion.2
  440.6 1.3 convolution_subtract_fusion
  441.9 11.7 %cholesky.217 = f32[128,128]{1,0:T(8,128)S(1)} custom-call(f32[128,128]{1,0:T(8,128)S(1)} %cholesky.270), custom_call_target="Cholesky" | custom-call | tf_op jit(solution)/shard_map/jit(cholesky)/cholesky | solution.py:42
  453.6 9.8 %custom-call.28 = f32[1,128,128]{1,2,0:T(8,128)S(1)} custom-call(f32[1,128,128]{2,1,0:T(8,128)S(1)} %get-tuple-element.16), custom_call_target="InvertDiagBlocksLowerTriangular" | custom-call | tf_op jit(solution)/shard_map/jit(cholesky)/cholesky | solution.py:42
  463.4 0.3 convolution_dynamic-update-slice_fusion
  463.7 1.3 convolution_subtract_fusion.1
  465.0 11.9 %cholesky.238 = f32[128,128]{1,0:T(8,128)S(1)} custom-call(f32[128,128]{1,0:T(8,128)S(1)} %cholesky.275), custom_call_target="Cholesky" | custom-call | tf_op jit(solution)/shard_map/jit(cholesky)/cholesky | solution.py:42
  476.9 0.7 compare_reduce_fusion.1
  477.6 9.8 %custom-call.29 = f32[1,128,128]{1,2,0:T(8,128)S(1)} custom-call(f32[1,128,128]{2,1,0:T(8,128)S(1)} %get-tuple-element.13), custom_call_target="InvertDiagBlocksLowerTriangular" | custom-call | tf_op jit(solution)/shard_map/jit(cholesky)/cholesky | solution.py:42
  487.6 1.2 convolution_subtract_fusion.2
  488.9 11.7 %cholesky.255 = f32[128,128]{1,0:T(8,128)S(1)} custom-call(f32[128,128]{1,0:T(8,128)S(1)} %convolution_subtract_fusion.2), custom_call_target="Cholesky" | custom-call | tf_op jit(solution)/shard_map/jit(cholesky)/cholesky | solution.py:42
  500.6 0.6 compare_reduce_fusion
  501.3 0.7 compare_reduce_fusion.2
  504.6 1.2 fusion.65
  505.8 4.7 gather_fusion
  510.5 2.1 fusion.20
  512.6 3.0 convolution_add_fusion.7
  515.6 1.8 fusion.21
  517.4 2.5 copy.32
  520.0 1.8 fusion.22
  521.8 1.8 convolution_add_fusion.6
  523.7 1.8 fusion.23
  525.5 1.8 convolution_add_fusion.5
  527.4 2.3 fusion.24
  529.7 1.9 convolution_add_fusion.4
  531.5 1.8 fusion.25
  533.4 1.8 convolution_add_fusion.3
  535.2 1.8 fusion.26
  537.1 1.9 convolution_add_fusion.2
  538.9 1.8 fusion.27
  540.8 2.0 convolution_add_fusion.1
  542.8 1.9 fusion.4
  544.7 8.3 %fusion.28 = f32[2048,512]{1,0:T(8,128)} fusion(f32[2048,512]{1,0:T(8,128)S(1)} %bitcast.82, f32[512,512]{1,0:T(8,128)S(1)} %fusion.4), kind=kOutput, calls=%fused_computation.77 | convolution fusion | flops 6442450944 | bytes 9437184 | tf_op jit(solution)/shard_map/dot_general | solution.py:8
  (31 shorter events, 1.7 us)
Async XLA Ops:
  7.2 405.3 %copy-start = (f32[512,512]{1,0:T(8,128)S(1)}, f32[512,512]{1,0:T(8,128)}, u32[]{:S(2)}) copy-start(f32[512,512]{1,0:T(8,128)} %param.9) | copy-start | bytes 3145732
  7.2 20.7 %copy-start.5 = (s32[2048]{0:T(1024)S(1)}, s32[2048]{0:T(1024)}, u32[]{:S(2)}) copy-start(s32[2048]{0:T(1024)} %param.8) | copy-start | bytes 24580
  7.2 20.9 %copy-start.6 = (s32[2048]{0:T(1024)S(1)}, s32[2048]{0:T(1024)}, u32[]{:S(2)}) copy-start(s32[2048]{0:T(1024)} %param.6) | copy-start | bytes 24580
  7.2 405.3 %all-reduce.3.cloned.1.call-start = ((), (), s32[]{:S(2)}) async-start(), calls=%async_computation.1 | async-start | bytes 2097152 | tf_op jit(solution)/shard_map/psum | solution.py:56
  149.9 2.0 copy-start.1
  416.1 1.0 copy-start.3
  515.6 6.2 %copy-start.4 = (f32[512,512]{1,0:T(8,128)S(1)}, f32[512,512]{1,0:T(8,128)}, u32[]{:S(2)}) copy-start(f32[512,512]{1,0:T(8,128)} %convolution_add_fusion.7) | copy-start | bytes 3145732
  540.8 3.9 copy-start.2
Sparse Core Ops, SparseCore 0:
  160.1 252.2 all-reduce.2
where the time goes:
time: 565 us; the launch traced here: 560 us
  waiting for transfers between devices  252 us (45%)
  other arithmetic  114 us (20%)
  blocking collectives  108 us (19%)
  matrix products  56.4 us (10%)
  between operations  17.1 us (3%)
  local copies, waits for them, and re-layouts  11.4 us (2%)
    psum x1, waiting for transfers between devices, reduce_gram(): summed = lax.psum(local_gram, ('rows', 'grp'))  252 us
    all_to_all x1, blocking collectives, regroup_rows(): lax.all_to_all(outgoing, 'rows', split_axis=0, concat_axis=0, tiled=True)  108 us
    another operation x14, other arithmetic, upper_factor(): return jnp.linalg.cholesky(matrix).T  79.1 us
    dot_general x18, matrix products, matmul(): jnp.dot(left, right, precision=lax.Precision.HIGHEST, preferred_element_t...  42.9 us
    another operation x3, other arithmetic  18.5 us
    scatter x1, other arithmetic, regroup_rows(): outgoing = jnp.zeros_like(values).at[target].set(values)  13 us
  transfers between devices with their start and end apart: 1, of which 1 were waited for; matrix products, arithmetic and copies ran while one was open for 0% of the time, Pallas kernels for 0%

commit v1 on v0

--- a/solution.py
+++ b/solution.py
@@ -2,6 +2,11 @@
 import jax.numpy as jnp
 from jax import lax
 from jax.sharding import PartitionSpec as P
+
+
+def one_after_other(value, one, other):
+    inner = lax.psum(value, one)
+    return lax.psum(inner, other)
 
 
 def matmul(left, right):
@@ -53,7 +58,7 @@
 
 
 def reduce_gram(local_gram, prior_gram, total_rows):
-    summed = lax.psum(local_gram, ("rows", "grp"))
+    summed = one_after_other(local_gram, "rows", "grp")
     return upper_factor(prior_gram + summed / jnp.float32(total_rows))
 
 

time: 565 us -> 545 us (0.965)
  waiting for transfers between devices: 252 us -> 233 us
    psum x1 -> x2, waiting for transfers between devices: 252 us -> 233 us  [the longest x1 182 us: one_after_other(): inner = lax.psum(value, one)]
  transfers between devices with their start and end apart: 1 -> 2, of which waited for: 1 -> 2; matrix products, arithmetic and copies ran while one was open for 0% -> 0% of each run, Pallas kernels for 0% -> 0%
where the time goes in v1:
time: 545 us; the launch traced here: 541 us
  waiting for transfers between devices  233 us (43%)
  other arithmetic  114 us (21%)
  blocking collectives  109 us (20%)
  matrix products  56.3 us (10%)
  between operations  17.4 us (3%)
  local copies, waits for them, and re-layouts  11.2 us (2%)
    psum x1, waiting for transfers between devices, one_after_other(): inner = lax.psum(value, one)  182 us
    all_to_all x1, blocking collectives, regroup_rows(): lax.all_to_all(outgoing, 'rows', split_axis=0, concat_axis=0, tiled=True)  109 us
    another operation x14, other arithmetic, upper_factor(): return jnp.linalg.cholesky(matrix).T  79 us
    psum x1, waiting for transfers between devices, one_after_other(): return lax.psum(inner, other)  51 us
    dot_general x18, matrix products, matmul(): jnp.dot(left, right, precision=lax.Precision.HIGHEST, preferred_element_t...  42.8 us
    another operation x3, other arithmetic  18.5 us
    scatter x1, other arithmetic, regroup_rows(): outgoing = jnp.zeros_like(values).at[target].set(values)  13 us
  transfers between devices with their start and end apart: 2, of which 2 were waited for; matrix products, arithmetic and copies ran while one was open for 0% of the time, Pallas kernels for 0%

profile of v1, /device:TPU:2, one launch (start us, length us, event | category | flops | bytes accessed | tf_op | source)
XLA Modules:
  0.0 540.7 jit_solution(14596436237308876592)
XLA Ops:
  7.2 0.7 broadcast_divide_fusion
  8.0 0.7 fusion.8
  8.7 18.1 %reduce-window.6 = s32[64,16,128]{2,1,0:T(8,128)S(1)} reduce-window(s32[64,16,128]{2,1,0:T(8,128)S(1)} %fusion.8, s32[]{:T(128)} %constant.151.clone.1), window={size=1x1x128 pad=0_0x0_0x127_0}, to_apply=%region_0.1 | reduce-window | flops 16646144 | bytes 1048580 | tf_op jit(solution)/shard_map/reduce-window
  27.1 0.4 copy.35
  28.1 0.6 select_reduce_fusion
  28.8 13.0 %scatter_custom_fusion = f32[2048,512]{1,0:T(8,128)} fusion(s32[2048]{0:T(1024)S(1)} %compare_select_fusion, f32[2048,512]{1,0:T(8,128)} %param.5, f32[2048]{0:T(1024)S(1)} %select_reduce_fusion, f32[]{:T(128)} %constant.149.clone.1), kind=kCustom, calls=%fused_computation.2 | custom fusion | flops 1048576 | bytes 8396804 | tf_op jit(solution)/shard_map/scatter | solution.py:56
  41.7 108.7 %all_to_all.12 = f32[64,32,512]{2,1,0:T(8,128)S(1)} all-to-all(f32[64,32,512]{2,1,0:T(8,128)} %bitcast.84), channel_id=1, replica_groups=mesh['rows'=64,'grp'=4] {'rows'}, dimensions={0} | all-to-all | bytes 8388608 | tf_op jit(solution)/shard_map/all_to_all | solution.py:57
  150.5 2.0 copy-done.1
  152.5 8.0 %convolution_bitcast_fusion = f32[512,512]{0,1:T(8,128)} fusion(f32[64,32,512]{2,1,0:T(8,128)S(1)} %all_to_all.12), kind=kOutput, calls=%fused_computation.17 | convolution fusion | flops 6442450944 | bytes 5242880 | tf_op jit(solution)/shard_map/dot_general | solution.py:17
  160.8 181.5 %all-reduce.4.cloned.1.call-done = f32[512,512]{0,1:T(8,128)} async-done(((f32[512,512]{0,1:T(8,128)}), f32[512,512]{0,1:T(8,128)}) %all-reduce.4.cloned.1.call-update) | async-done | bytes 1048592 | tf_op jit(solution)/shard_map/psum | solution.py:8
  342.3 51.0 %all-reduce.6.cloned.1.call-done = f32[512,512]{0,1:T(8,128)} async-done(((f32[512,512]{0,1:T(8,128)}), f32[512,512]{0,1:T(8,128)}) %all-reduce.6.cloned.1.call-update) | async-done | bytes 1048592 | tf_op jit(solution)/shard_map/psum | solution.py:9
  393.3 3.1 convolution_add_fusion.8
  396.4 0.3 copy.31
  397.0 1.0 copy-done.3
  398.0 11.7 %cholesky.104 = f32[128,128]{1,0:T(8,128)S(1)} custom-call(f32[128,128]{1,0:T(8,128)S(1)} %cholesky.266), custom_call_target="Cholesky" | custom-call | tf_op jit(solution)/shard_map/jit(cholesky)/cholesky | solution.py:47
  409.9 9.8 %custom-call.27 = f32[1,128,128]{1,2,0:T(8,128)S(1)} custom-call(f32[1,128,128]{2,1,0:T(8,128)S(1)} %get-tuple-element.19), custom_call_target="InvertDiagBlocksLowerTriangular" | custom-call | tf_op jit(solution)/shard_map/jit(cholesky)/cholesky | solution.py:47
  419.7 1.2 constant_dynamic-update-slice_fusion.2
  420.9 1.3 convolution_subtract_fusion
  422.2 12.1 %cholesky.217 = f32[128,128]{1,0:T(8,128)S(1)} custom-call(f32[128,128]{1,0:T(8,128)S(1)} %cholesky.270), custom_call_target="Cholesky" | custom-call | tf_op jit(solution)/shard_map/jit(cholesky)/cholesky | solution.py:47
  434.3 9.8 %custom-call.28 = f32[1,128,128]{1,2,0:T(8,128)S(1)} custom-call(f32[1,128,128]{2,1,0:T(8,128)S(1)} %get-tuple-element.16), custom_call_target="InvertDiagBlocksLowerTriangular" | custom-call | tf_op jit(solution)/shard_map/jit(cholesky)/cholesky | solution.py:47
  444.4 1.3 convolution_subtract_fusion.1
  445.7 11.7 %cholesky.238 = f32[128,128]{1,0:T(8,128)S(1)} custom-call(f32[128,128]{1,0:T(8,128)S(1)} %cholesky.275), custom_call_target="Cholesky" | custom-call | tf_op jit(solution)/shard_map/jit(cholesky)/cholesky | solution.py:47
  457.5 0.7 compare_reduce_fusion.1
  458.2 9.8 %custom-call.29 = f32[1,128,128]{1,2,0:T(8,128)S(1)} custom-call(f32[1,128,128]{2,1,0:T(8,128)S(1)} %get-tuple-element.13), custom_call_target="InvertDiagBlocksLowerTriangular" | custom-call | tf_op jit(solution)/shard_map/jit(cholesky)/cholesky | solution.py:47
  468.2 1.2 convolution_subtract_fusion.2
  469.5 11.9 %cholesky.255 = f32[128,128]{1,0:T(8,128)S(1)} custom-call(f32[128,128]{1,0:T(8,128)S(1)} %convolution_subtract_fusion.2), custom_call_target="Cholesky" | custom-call | tf_op jit(solution)/shard_map/jit(cholesky)/cholesky | solution.py:47
  481.4 0.6 compare_reduce_fusion
  482.0 0.7 compare_reduce_fusion.2
  485.3 1.2 fusion.65
  486.5 4.5 gather_fusion
  491.0 2.1 fusion.20
  493.1 3.0 convolution_add_fusion.7
  496.1 1.8 fusion.21
  497.9 2.5 copy.32
  500.5 1.8 fusion.22
  502.3 1.8 convolution_add_fusion.6
  504.2 1.8 fusion.23
  506.0 1.8 convolution_add_fusion.5
  507.9 2.1 fusion.24
  510.0 1.8 convolution_add_fusion.4
  511.8 1.8 fusion.25
  513.7 1.8 convolution_add_fusion.3
  515.5 1.8 fusion.26
  517.4 1.8 convolution_add_fusion.2
  519.2 1.8 fusion.27
  521.1 2.1 convolution_add_fusion.1
  523.2 1.9 fusion.4
  525.1 8.3 %fusion.28 = f32[2048,512]{1,0:T(8,128)} fusion(f32[2048,512]{1,0:T(8,128)S(1)} %bitcast.82, f32[512,512]{1,0:T(8,128)S(1)} %fusion.4), kind=kOutput, calls=%fused_computation.77 | convolution fusion | flops 6442450944 | bytes 9437184 | tf_op jit(solution)/shard_map/dot_general | solution.py:13
  (34 shorter events, 2.2 us)
Async XLA Ops:
  7.2 386.2 %copy-start = (f32[512,512]{1,0:T(8,128)S(1)}, f32[512,512]{1,0:T(8,128)}, u32[]{:S(2)}) copy-start(f32[512,512]{1,0:T(8,128)} %param.9) | copy-start | bytes 3145732
  7.2 20.7 %copy-start.5 = (s32[2048]{0:T(1024)S(1)}, s32[2048]{0:T(1024)}, u32[]{:S(2)}) copy-start(s32[2048]{0:T(1024)} %param.8) | copy-start | bytes 24580
  7.2 20.9 %copy-start.6 = (s32[2048]{0:T(1024)S(1)}, s32[2048]{0:T(1024)}, u32[]{:S(2)}) copy-start(s32[2048]{0:T(1024)} %param.6) | copy-start | bytes 24580
  7.2 335.1 %all-reduce.4.cloned.1.call-start = ((), (), s32[]{:S(2)}) async-start(), calls=%async_computation.1 | async-start | bytes 2097152 | tf_op jit(solution)/shard_map/psum | solution.py:8
  150.5 2.0 copy-start.1
  160.5 232.8 %all-reduce.6.cloned.1.call-start = ((), (), s32[]{:S(2)}) async-start(), calls=%async_computation.2 | async-start | bytes 2097152 | tf_op jit(solution)/shard_map/psum | solution.py:9
  397.0 1.0 copy-start.3
  496.1 6.2 %copy-start.4 = (f32[512,512]{1,0:T(8,128)S(1)}, f32[512,512]{1,0:T(8,128)}, u32[]{:S(2)}) copy-start(f32[512,512]{1,0:T(8,128)} %convolution_add_fusion.7) | copy-start | bytes 3145732
  521.1 4.0 copy-start.2
Sparse Core Ops, SparseCore 0:
  160.7 181.6 all-reduce.3
  344.8 48.4 all-reduce.5
